TPU v7x, 128 devices: a whole 4x4x4 slice. The times are simulated.
128 devices in a mesh: cfg: 2 (over core), req: 4 (over y), seq: 16 (over z, x).
Axes of the slice: x: 4, y: 4, z: 4, core: 2. Of those that a mesh axis runs over, the one named last changes fastest.
Arguments:
- img_qkv: bfloat16 [2, 8, 4096, 6144], P('cfg', 'req', 'seq'), may hold values from -4.5 to 4.5
- txt_kv: bfloat16 [2, 8, 512, 4096], P('cfg', 'req', 'seq'), may hold values from -4.5 to 4.5
- text_len: int32 [8], P('req'), may hold values from 77 to 512
- t_index: int32 [8], P('req'), may hold values from 0 to 3
- guidance: float32 [8], P('req'), may hold values from 1.5 to 6
- modulation: float32 [2, 8, 3, 3072], P('cfg', 'req'), may hold values from -4 to 4
- img_hidden: bfloat16 [2, 8, 4096, 3072], P('cfg', 'req', 'seq'), may hold values from -6 to 6
- latents: float32 [8, 4096, 64], P('req', 'seq', 'cfg'), may hold values from -6 to 6
- proj_weight: bfloat16 [2048, 3072], P(('cfg', 'req', 'seq')), may hold values from -0.125 to 0.125
- final_weight: bfloat16 [3072, 64], replicated, may hold values from -0.109375 to 0.109375
Outputs:
- latents_next: float32 [8, 4096, 64], P('req', 'seq', 'cfg')
- vel_norm: float32 [2, 8], P('cfg', 'req')
- max_logit: float32 [2, 8], P('cfg', 'req')
All inputs are finite; a program needn't handle non-finite values.
Results may differ from a plain program's by a relative error of at most 0.0033.
Values may be sent and summed in bfloat16 or wider, within the bound.
A program may use at most 128 MiB of HBM per device.

v0:
```python
import math
import jax
import jax.numpy as jnp
from jax import lax
from jax.sharding import PartitionSpec as P

HEADS = 16
HD = 128
STEPS = 4
time_shift = 1.15
norm_eps = 1e-06


def swapped(value, axis, stride):
    return lax.ppermute(value, axis, [(i, i ^ 1 << stride) for i in range(lax.axis_size(axis))])


def sigma_of(step_index):
    fraction = 1.0 - step_index.astype(jnp.float32) / STEPS
    lifted = fraction * math.exp(time_shift)
    return lifted / (lifted + 1.0 - fraction)


def shards(
    img_qkv,
    txt_kv,
    text_len,
    t_index,
    guidance,
    modulation,
    img_hidden,
    latents,
    proj_weight,
    final_weight,
):
    local_prompts = img_qkv.shape[1]
    img_dev = img_qkv.shape[2]
    txt_dev = txt_kv.shape[2]
    joined = img_qkv[0].reshape(local_prompts, img_dev, 3, HEADS, HD)
    text_rows = txt_kv[0].reshape(local_prompts, txt_dev, 2, HEADS, HD)
    full_img, full_txt = (
        lax.all_to_all(joined, "seq", split_axis=3, concat_axis=1, tiled=True),
        lax.all_to_all(text_rows, "seq", split_axis=3, concat_axis=1, tiled=True),
    )
    img_len = full_img.shape[1]
    txt_len = full_txt.shape[1]
    local_heads = full_img.shape[3]
    block_rows = math.gcd(img_len, 1024)
    mixed_list = []
    max_list = []
    for prompt in range(local_prompts):
        key_rows = jnp.concatenate([full_txt[prompt, :, 0], full_img[prompt, :, 1]], axis=0)
        value_rows = jnp.concatenate([full_txt[prompt, :, 1], full_img[prompt, :, 2]], axis=0)
        key_valid = jnp.concatenate(
            [jnp.arange(txt_len) < text_len[prompt], jnp.ones((img_len,), jnp.bool_)]
        )

        def one_block(query_rows):
            logits = jnp.einsum(
                "qhd,khd->hqk", query_rows, key_rows, preferred_element_type=jnp.float32
            ) * HD ** (-0.5)
            logits = jnp.where(key_valid[None, None, :], logits, -jnp.inf)
            row_max = jnp.max(logits, axis=2, keepdims=True)
            weights = jnp.exp(logits - row_max)
            weights = (weights / jnp.sum(weights, axis=2, keepdims=True)).astype(jnp.bfloat16)
            mixed_rows = jnp.einsum(
                "hqk,khd->qhd", weights, value_rows, preferred_element_type=jnp.float32
            ).astype(jnp.bfloat16)
            return (mixed_rows, jnp.max(row_max))

        mixed_rows, top_logit = lax.map(
            one_block,
            full_img[prompt, :, 0].reshape(img_len // block_rows, block_rows, local_heads, HD),
        )
        mixed_list.append(mixed_rows.reshape(img_len, local_heads, HD))
        max_list.append(jnp.max(top_logit))
    local_max = jnp.stack(max_list)
    head_rows = jnp.stack(mixed_list)
    token_rows = lax.all_to_all(head_rows, "seq", split_axis=1, concat_axis=2, tiled=True)
    attended = token_rows.reshape(local_prompts * img_dev, HEADS * HD)
    projected = jnp.dot(
        attended,
        lax.all_gather(proj_weight, ("cfg", "req", "seq"), axis=0, tiled=True),
        preferred_element_type=jnp.float32,
    )
    projected = projected.reshape(local_prompts, img_dev, projected.shape[1])
    mod_rows = modulation[0]
    hidden = img_hidden[0].astype(jnp.float32) + mod_rows[:, 0][:, None, :] * projected
    average = jnp.mean(hidden, axis=2, keepdims=True)
    centred = hidden - average
    variance = jnp.mean(centred * centred, axis=2, keepdims=True)
    normed = (
        centred / jnp.sqrt(variance + norm_eps) * (1.0 + mod_rows[:, 1][:, None, :])
        + mod_rows[:, 2][:, None, :]
    ).astype(jnp.bfloat16)
    velocity = jnp.einsum("ptd,dc->ptc", normed, final_weight, preferred_element_type=jnp.float32)
    half_chan = latents.shape[2]
    copy_pos = lax.axis_index("cfg")
    own_part = lax.dynamic_slice_in_dim(velocity, copy_pos * half_chan, half_chan, 2)
    other_part = lax.dynamic_slice_in_dim(velocity, (1 - copy_pos) * half_chan, half_chan, 2)
    partner = swapped(other_part, "cfg", 0)
    is_cond = copy_pos == 0
    cond_vel = jnp.where(is_cond, own_part, partner)
    uncond_vel = jnp.where(is_cond, partner, own_part)
    guided = uncond_vel + guidance[:, None, None] * (cond_vel - uncond_vel)
    square_sum = jnp.sum(guided * guided, axis=(1, 2))
    total_sq = lax.psum(square_sum, "seq")
    global_max = lax.pmax(local_max, "seq")
    vel_norm = jnp.sqrt(total_sq / (img_len * half_chan) + norm_eps)
    euler_step = sigma_of(t_index + 1) - sigma_of(t_index)
    advanced = latents + euler_step[:, None, None] * guided
    return (advanced, vel_norm.reshape(1, local_prompts), global_max.reshape(1, local_prompts))


def solution(mesh):
    return jax.shard_map(
        shards,
        mesh=mesh,
        in_specs=(
            P("cfg", "req", "seq", None),
            P("cfg", "req", "seq", None),
            P("req"),
            P("req"),
            P("req"),
            P("cfg", "req", None, None),
            P("cfg", "req", "seq", None),
            P("req", "seq", "cfg"),
            P(("cfg", "req", "seq"), None),
            P(),
        ),
        out_specs=(P("req", "seq", "cfg"), P("cfg", "req"), P("cfg", "req")),
        check_vma=False,
    )
```

profile of v0, /device:TPU:24, one launch (start us, length us, event | category | flops | bytes accessed | tf_op | source)
XLA Modules:
  0.0 548.9 jit_solution(1137736579929246898)
XLA Ops:
  7.2 1.2 copy.41
  8.4 1.0 copy.34
  9.4 7.9 %all-to-all-start.1 = ((bf16[2,32,2,16,128]{4,1,2,0,3:T(8,128)(2,1)}), bf16[2,32,2,16,128]{4,1,2,0,3:T(8,128)(2,1)S(1)}, u32[]{:S(2)}, u32[]{:S(2)}) async-start(bf16[2,32,2,16,128]{4,1,2,0,3:T(8,128)(2,1)} %copy.34), calls=%async_computation.1 | async-start | bytes 1048576 | tf_op jit(solution)/shard_map/all_to_all | solution.py:43
  17.3 8.6 %copy.31 = bf16[1,2,256,6144]{2,3,1,0:T(8,128)(2,1)} copy(bf16[1,2,256,6144]{3,2,1,0:T(8,128)(2,1)} %param.14) | data formatting | bytes 12582912 | tf_op args[0]
  25.9 8.7 %copy.32 = bf16[2,256,3,16,128]{4,1,2,0,3:T(8,128)(2,1)} copy(bf16[2,256,3,16,128]{1,4,3,2,0:T(8,128)(2,1)} %bitcast.151) | data formatting | bytes 12582912 | tf_op jit(solution)/shard_map/reshape;squeeze | solution.py:39
  34.6 7.4 %all-to-all-start = ((bf16[2,256,3,16,128]{4,1,2,0,3:T(8,128)(2,1)}), bf16[2,256,3,16,128]{4,1,2,0,3:T(8,128)(2,1)}, u32[]{:S(2)}, u32[]{:S(2)}) async-start(bf16[2,256,3,16,128]{4,1,2,0,3:T(8,128)(2,1)} %copy.32), calls=%async_computation | async-start | bytes 12582912 | tf_op jit(solution)/shard_map/all_to_all | solution.py:42
  42.1 0.7 all-gather.2.cloned.1.call-update
  43.3 0.6 iota_compare_fusion.1
  44.0 0.7 iota_compare_fusion
  45.3 0.8 slice_bitcast_fusion.6
  46.1 93.6 %all-to-all-done = bf16[2,256,3,16,128]{4,1,2,0,3:T(8,128)(2,1)} async-done(((bf16[2,256,3,16,128]{4,1,2,0,3:T(8,128)(2,1)}), bf16[2,256,3,16,128]{4,1,2,0,3:T(8,128)(2,1)}, u32[]{:S(2)}, u32[]{:S(2)}) %all-to-all-start) | async-done | bytes 6291488 | tf_op jit(solution)/shard_map/all_to_all | solution.py:42
  139.7 3.2 copy.33
  142.9 1.7 slice_bitcast_fusion.2
  144.7 1.2 pad_maximum_fusion.1
  145.9 1.1 broadcast.86.clone.1
  147.0 122.4 %while.24 = (s32[]{:T(128)}, bf16[4,1024,1,128]{3,1,2,0:T(8,128)(2,1)}, f32[4]{0:T(128)S(1)}, pred[4608]{0:T(1024)(128)(4,1)S(1)}, bf16[4,1024,1,128]{3,1,2,0:T(...) while((s32[]{:T(128)}, ...), condition=%wide.region_4.5_spmd, body=%wide.region_0.4_spmd.sunk | while | flops 2477389824 | bytes 59542120 | solution.py:71
  147.0 8.2 %fusion.57 = (f32[1024]{0:T(1024)S(1)}, f32[1024,4608]{1,0:T(8,128)}) fusion(pred[4608]{0:T(1024)(128)(4,1)S(1)} %get-tuple-element.343, bf16[4608,1,128]{2,0,1:T(8,128)(2,1)S(1)} %get-tuple-element.345, bf16[4,1024,1,128]{3,1,2,0:T(8,128)(2,1)S(1)} %get-tuple-element.344, s32[]{:T(128)} %get-tuple-element.332), kind=kOutput, calls=%fused_computation.5.clone.1 | convolution fusion | flops 1222114304 | bytes 20325380 | tf_op jit(solution)/shard_map/while/body/eval_jaxpr/qhd,khd->hqk/dot_general | solution.py:59
  155.2 13.3 %fusion.58 = (f32[]{:T(128)}, f32[1024]{0:T(1024)S(1)}) fusion(f32[1024,4608]{1,0:T(8,128)} %get-tuple-element.285, pred[4608]{0:T(1024)(128)(4,1)S(1)} %get-tuple-element.343, f32[1024]{0:T(1024)S(1)} %get-tuple-element.286), kind=kLoop, calls=%fused_computation.4.clone.1 | loop fusion | flops 23591936 | bytes 18887172 | tf_op jit(solution)/shard_map/while/body/eval_jaxpr/reduce_max | solution.py:69
  168.5 9.6 %fusion.59 = bf16[4,1024,1,128]{3,1,2,0:T(8,128)(2,1)} fusion(bf16[4,1024,1,128]{3,1,2,0:T(8,128)(2,1)} %get-tuple-element.333, s32[]{:T(128)} %get-tuple-element.332, bf16[4608,1,128]{2,0,1:T(8,128)(2,1)} %get-tuple-element.346, f32[1024,4608]{1,0:T(8,128)} %get-tuple-element.285, f32[1024]{0:T(1024)S(1)} %get-tuple-element.287, ...), kind=kOutput, calls=%fused_computation.12.clone.1 | convolution fusion | flops 1231683584 | bytes 20329472 | tf_op jit(solution)/shard_map/while/body/eval_jaxpr/hqk,khd->qhd/dot_general | solution.py:66
  178.0 0.8 dynamic_update_slice.21
  178.8 7.9 %fusion.57 = (f32[1024]{0:T(1024)S(1)}, f32[1024,4608]{1,0:T(8,128)}) fusion(pred[4608]{0:T(1024)(128)(4,1)S(1)} %get-tuple-element.343, bf16[4608,1,128]{2,0,1:T(8,128)(2,1)S(1)} %get-tuple-element.345, bf16[4,1024,1,128]{3,1,2,0:T(8,128)(2,1)S(1)} %get-tuple-element.344, s32[]{:T(128)} %get-tuple-element.332), kind=kOutput, calls=%fused_computation.5.clone.1 | convolution fusion | flops 1222114304 | bytes 20325380 | tf_op jit(solution)/shard_map/while/body/eval_jaxpr/qhd,khd->hqk/dot_general | solution.py:59
  186.7 12.0 %fusion.58 = (f32[]{:T(128)}, f32[1024]{0:T(1024)S(1)}) fusion(f32[1024,4608]{1,0:T(8,128)} %get-tuple-element.285, pred[4608]{0:T(1024)(128)(4,1)S(1)} %get-tuple-element.343, f32[1024]{0:T(1024)S(1)} %get-tuple-element.286), kind=kLoop, calls=%fused_computation.4.clone.1 | loop fusion | flops 23591936 | bytes 18887172 | tf_op jit(solution)/shard_map/while/body/eval_jaxpr/reduce_max | solution.py:69
  198.7 9.6 %fusion.59 = bf16[4,1024,1,128]{3,1,2,0:T(8,128)(2,1)} fusion(bf16[4,1024,1,128]{3,1,2,0:T(8,128)(2,1)} %get-tuple-element.333, s32[]{:T(128)} %get-tuple-element.332, bf16[4608,1,128]{2,0,1:T(8,128)(2,1)} %get-tuple-element.346, f32[1024,4608]{1,0:T(8,128)} %get-tuple-element.285, f32[1024]{0:T(1024)S(1)} %get-tuple-element.287, ...), kind=kOutput, calls=%fused_computation.12.clone.1 | convolution fusion | flops 1231683584 | bytes 20329472 | tf_op jit(solution)/shard_map/while/body/eval_jaxpr/hqk,khd->qhd/dot_general | solution.py:66
  208.3 0.8 dynamic_update_slice.21
  209.0 7.9 %fusion.57 = (f32[1024]{0:T(1024)S(1)}, f32[1024,4608]{1,0:T(8,128)}) fusion(pred[4608]{0:T(1024)(128)(4,1)S(1)} %get-tuple-element.343, bf16[4608,1,128]{2,0,1:T(8,128)(2,1)S(1)} %get-tuple-element.345, bf16[4,1024,1,128]{3,1,2,0:T(8,128)(2,1)S(1)} %get-tuple-element.344, s32[]{:T(128)} %get-tuple-element.332), kind=kOutput, calls=%fused_computation.5.clone.1 | convolution fusion | flops 1222114304 | bytes 20325380 | tf_op jit(solution)/shard_map/while/body/eval_jaxpr/qhd,khd->hqk/dot_general | solution.py:59
  216.9 12.0 %fusion.58 = (f32[]{:T(128)}, f32[1024]{0:T(1024)S(1)}) fusion(f32[1024,4608]{1,0:T(8,128)} %get-tuple-element.285, pred[4608]{0:T(1024)(128)(4,1)S(1)} %get-tuple-element.343, f32[1024]{0:T(1024)S(1)} %get-tuple-element.286), kind=kLoop, calls=%fused_computation.4.clone.1 | loop fusion | flops 23591936 | bytes 18887172 | tf_op jit(solution)/shard_map/while/body/eval_jaxpr/reduce_max | solution.py:69
  228.9 9.6 %fusion.59 = bf16[4,1024,1,128]{3,1,2,0:T(8,128)(2,1)} fusion(bf16[4,1024,1,128]{3,1,2,0:T(8,128)(2,1)} %get-tuple-element.333, s32[]{:T(128)} %get-tuple-element.332, bf16[4608,1,128]{2,0,1:T(8,128)(2,1)} %get-tuple-element.346, f32[1024,4608]{1,0:T(8,128)} %get-tuple-element.285, f32[1024]{0:T(1024)S(1)} %get-tuple-element.287, ...), kind=kOutput, calls=%fused_computation.12.clone.1 | convolution fusion | flops 1231683584 | bytes 20329472 | tf_op jit(solution)/shard_map/while/body/eval_jaxpr/hqk,khd->qhd/dot_general | solution.py:66
  238.4 0.8 dynamic_update_slice.21
  239.2 7.9 %fusion.57 = (f32[1024]{0:T(1024)S(1)}, f32[1024,4608]{1,0:T(8,128)}) fusion(pred[4608]{0:T(1024)(128)(4,1)S(1)} %get-tuple-element.343, bf16[4608,1,128]{2,0,1:T(8,128)(2,1)S(1)} %get-tuple-element.345, bf16[4,1024,1,128]{3,1,2,0:T(8,128)(2,1)S(1)} %get-tuple-element.344, s32[]{:T(128)} %get-tuple-element.332), kind=kOutput, calls=%fused_computation.5.clone.1 | convolution fusion | flops 1222114304 | bytes 20325380 | tf_op jit(solution)/shard_map/while/body/eval_jaxpr/qhd,khd->hqk/dot_general | solution.py:59
  247.1 12.0 %fusion.58 = (f32[]{:T(128)}, f32[1024]{0:T(1024)S(1)}) fusion(f32[1024,4608]{1,0:T(8,128)} %get-tuple-element.285, pred[4608]{0:T(1024)(128)(4,1)S(1)} %get-tuple-element.343, f32[1024]{0:T(1024)S(1)} %get-tuple-element.286), kind=kLoop, calls=%fused_computation.4.clone.1 | loop fusion | flops 23591936 | bytes 18887172 | tf_op jit(solution)/shard_map/while/body/eval_jaxpr/reduce_max | solution.py:69
  259.1 9.6 %fusion.59 = bf16[4,1024,1,128]{3,1,2,0:T(8,128)(2,1)} fusion(bf16[4,1024,1,128]{3,1,2,0:T(8,128)(2,1)} %get-tuple-element.333, s32[]{:T(128)} %get-tuple-element.332, bf16[4608,1,128]{2,0,1:T(8,128)(2,1)} %get-tuple-element.346, f32[1024,4608]{1,0:T(8,128)} %get-tuple-element.285, f32[1024]{0:T(1024)S(1)} %get-tuple-element.287, ...), kind=kOutput, calls=%fused_computation.12.clone.1 | convolution fusion | flops 1231683584 | bytes 20329472 | tf_op jit(solution)/shard_map/while/body/eval_jaxpr/hqk,khd->qhd/dot_general | solution.py:66
  268.6 0.8 dynamic_update_slice.21
  269.4 2.7 pad_maximum_fusion.3
  272.3 122.5 %while.25 = (s32[]{:T(128)}, bf16[4,1024,1,128]{3,1,2,0:T(8,128)(2,1)S(1)}, f32[4]{0:T(128)S(1)}, pred[4608]{0:T(1024)(128)(4,1)S(1)}, bf16[4,1024,1,128]{3,1,2,...) while((s32[]{:T(128)}, ...), condition=%wide.region_9.10_spmd, body=%wide.region_5.9_spmd.sunk | while | flops 2477389824 | bytes 59542120 | solution.py:71
  272.5 8.9 %fusion.61 = (f32[1024]{0:T(1024)S(1)}, f32[1024,4608]{1,0:T(8,128)}) fusion(pred[4608]{0:T(1024)(128)(4,1)S(1)} %get-tuple-element.319, bf16[4608,1,128]{2,0,1:T(8,128)(2,1)S(1)} %get-tuple-element.321, bf16[4,1024,1,128]{3,1,2,0:T(8,128)(2,1)} %get-tuple-element.320, s32[]{:T(128)} %get-tuple-element.308), kind=kOutput, calls=%fused_computation.23.clone.1 | convolution fusion | flops 1222114304 | bytes 20325376 | tf_op jit(solution)/shard_map/while/body/eval_jaxpr/qhd,khd->hqk/dot_general | solution.py:59
  281.3 12.0 %fusion.62 = (f32[]{:T(128)}, f32[1024]{0:T(1024)S(1)}) fusion(f32[1024,4608]{1,0:T(8,128)} %get-tuple-element.296, pred[4608]{0:T(1024)(128)(4,1)S(1)} %get-tuple-element.319, f32[1024]{0:T(1024)S(1)} %get-tuple-element.297), kind=kLoop, calls=%fused_computation.22.clone.1 | loop fusion | flops 23591936 | bytes 18887172 | tf_op jit(solution)/shard_map/while/body/eval_jaxpr/reduce_max | solution.py:69
  293.3 9.0 %fusion.63 = bf16[4,1024,1,128]{3,1,2,0:T(8,128)(2,1)S(1)} fusion(bf16[4,1024,1,128]{3,1,2,0:T(8,128)(2,1)S(1)} %get-tuple-element.309, s32[]{:T(128)} %get-tuple-element.308, bf16[4608,1,128]{2,0,1:T(8,128)(2,1)} %get-tuple-element.322, f32[1024,4608]{1,0:T(8,128)} %get-tuple-element.296, f32[1024]{0:T(1024)S(1)} %get-tuple-element.298, ...), kind=kOutput, calls=%fused_computation.30.clone.1 | convolution fusion | flops 1231683584 | bytes 20329476 | tf_op jit(solution)/shard_map/while/body/eval_jaxpr/hqk,khd->qhd/dot_general | solution.py:66
  302.3 0.8 dynamic_update_slice.23
  303.1 8.8 %fusion.61 = (f32[1024]{0:T(1024)S(1)}, f32[1024,4608]{1,0:T(8,128)}) fusion(pred[4608]{0:T(1024)(128)(4,1)S(1)} %get-tuple-element.319, bf16[4608,1,128]{2,0,1:T(8,128)(2,1)S(1)} %get-tuple-element.321, bf16[4,1024,1,128]{3,1,2,0:T(8,128)(2,1)} %get-tuple-element.320, s32[]{:T(128)} %get-tuple-element.308), kind=kOutput, calls=%fused_computation.23.clone.1 | convolution fusion | flops 1222114304 | bytes 20325376 | tf_op jit(solution)/shard_map/while/body/eval_jaxpr/qhd,khd->hqk/dot_general | solution.py:59
  311.9 12.0 %fusion.62 = (f32[]{:T(128)}, f32[1024]{0:T(1024)S(1)}) fusion(f32[1024,4608]{1,0:T(8,128)} %get-tuple-element.296, pred[4608]{0:T(1024)(128)(4,1)S(1)} %get-tuple-element.319, f32[1024]{0:T(1024)S(1)} %get-tuple-element.297), kind=kLoop, calls=%fused_computation.22.clone.1 | loop fusion | flops 23591936 | bytes 18887172 | tf_op jit(solution)/shard_map/while/body/eval_jaxpr/reduce_max | solution.py:69
  323.9 9.0 %fusion.63 = bf16[4,1024,1,128]{3,1,2,0:T(8,128)(2,1)S(1)} fusion(bf16[4,1024,1,128]{3,1,2,0:T(8,128)(2,1)S(1)} %get-tuple-element.309, s32[]{:T(128)} %get-tuple-element.308, bf16[4608,1,128]{2,0,1:T(8,128)(2,1)} %get-tuple-element.322, f32[1024,4608]{1,0:T(8,128)} %get-tuple-element.296, f32[1024]{0:T(1024)S(1)} %get-tuple-element.298, ...), kind=kOutput, calls=%fused_computation.30.clone.1 | convolution fusion | flops 1231683584 | bytes 20329476 | tf_op jit(solution)/shard_map/while/body/eval_jaxpr/hqk,khd->qhd/dot_general | solution.py:66
  332.9 0.8 dynamic_update_slice.23
  333.6 8.8 %fusion.61 = (f32[1024]{0:T(1024)S(1)}, f32[1024,4608]{1,0:T(8,128)}) fusion(pred[4608]{0:T(1024)(128)(4,1)S(1)} %get-tuple-element.319, bf16[4608,1,128]{2,0,1:T(8,128)(2,1)S(1)} %get-tuple-element.321, bf16[4,1024,1,128]{3,1,2,0:T(8,128)(2,1)} %get-tuple-element.320, s32[]{:T(128)} %get-tuple-element.308), kind=kOutput, calls=%fused_computation.23.clone.1 | convolution fusion | flops 1222114304 | bytes 20325376 | tf_op jit(solution)/shard_map/while/body/eval_jaxpr/qhd,khd->hqk/dot_general | solution.py:59
  342.5 12.0 %fusion.62 = (f32[]{:T(128)}, f32[1024]{0:T(1024)S(1)}) fusion(f32[1024,4608]{1,0:T(8,128)} %get-tuple-element.296, pred[4608]{0:T(1024)(128)(4,1)S(1)} %get-tuple-element.319, f32[1024]{0:T(1024)S(1)} %get-tuple-element.297), kind=kLoop, calls=%fused_computation.22.clone.1 | loop fusion | flops 23591936 | bytes 18887172 | tf_op jit(solution)/shard_map/while/body/eval_jaxpr/reduce_max | solution.py:69
  354.5 9.0 %fusion.63 = bf16[4,1024,1,128]{3,1,2,0:T(8,128)(2,1)S(1)} fusion(bf16[4,1024,1,128]{3,1,2,0:T(8,128)(2,1)S(1)} %get-tuple-element.309, s32[]{:T(128)} %get-tuple-element.308, bf16[4608,1,128]{2,0,1:T(8,128)(2,1)} %get-tuple-element.322, f32[1024,4608]{1,0:T(8,128)} %get-tuple-element.296, f32[1024]{0:T(1024)S(1)} %get-tuple-element.298, ...), kind=kOutput, calls=%fused_computation.30.clone.1 | convolution fusion | flops 1231683584 | bytes 20329476 | tf_op jit(solution)/shard_map/while/body/eval_jaxpr/hqk,khd->qhd/dot_general | solution.py:66
  363.5 0.8 dynamic_update_slice.23
  364.2 8.8 %fusion.61 = (f32[1024]{0:T(1024)S(1)}, f32[1024,4608]{1,0:T(8,128)}) fusion(pred[4608]{0:T(1024)(128)(4,1)S(1)} %get-tuple-element.319, bf16[4608,1,128]{2,0,1:T(8,128)(2,1)S(1)} %get-tuple-element.321, bf16[4,1024,1,128]{3,1,2,0:T(8,128)(2,1)} %get-tuple-element.320, s32[]{:T(128)} %get-tuple-element.308), kind=kOutput, calls=%fused_computation.23.clone.1 | convolution fusion | flops 1222114304 | bytes 20325376 | tf_op jit(solution)/shard_map/while/body/eval_jaxpr/qhd,khd->hqk/dot_general | solution.py:59
  373.0 12.0 %fusion.62 = (f32[]{:T(128)}, f32[1024]{0:T(1024)S(1)}) fusion(f32[1024,4608]{1,0:T(8,128)} %get-tuple-element.296, pred[4608]{0:T(1024)(128)(4,1)S(1)} %get-tuple-element.319, f32[1024]{0:T(1024)S(1)} %get-tuple-element.297), kind=kLoop, calls=%fused_computation.22.clone.1 | loop fusion | flops 23591936 | bytes 18887172 | tf_op jit(solution)/shard_map/while/body/eval_jaxpr/reduce_max | solution.py:69
  385.0 9.0 %fusion.63 = bf16[4,1024,1,128]{3,1,2,0:T(8,128)(2,1)S(1)} fusion(bf16[4,1024,1,128]{3,1,2,0:T(8,128)(2,1)S(1)} %get-tuple-element.309, s32[]{:T(128)} %get-tuple-element.308, bf16[4608,1,128]{2,0,1:T(8,128)(2,1)} %get-tuple-element.322, f32[1024,4608]{1,0:T(8,128)} %get-tuple-element.296, f32[1024]{0:T(1024)S(1)} %get-tuple-element.298, ...), kind=kOutput, calls=%fused_computation.30.clone.1 | convolution fusion | flops 1231683584 | bytes 20329476 | tf_op jit(solution)/shard_map/while/body/eval_jaxpr/hqk,khd->qhd/dot_general | solution.py:66
  394.0 0.8 dynamic_update_slice.23
  394.8 1.5 pad_maximum_fusion
  396.2 18.4 %copy.38 = bf16[2,4096,1,128]{3,0,2,1:T(2,128)(2,1)} copy(bf16[2,4096,1,128]{3,1,2,0:T(8,128)(2,1)S(1)} %pad_maximum_fusion) | data formatting | bytes 4194304 | tf_op jit(solution)/shard_map/stack | solution.py:78
  414.6 5.3 all-to-all-start.2
  420.0 0.6 reduce_max.54
  421.2 27.4 %all-to-all-done.2 = bf16[2,4096,1,128]{3,0,2,1:T(2,128)(2,1)S(1)} async-done(((bf16[2,4096,1,128]{3,0,2,1:T(2,128)(2,1)}), bf16[2,4096,1,128]{3,0,2,1:T(2,128)(2,1)S(1)}, u32[]{:S(2)}, u32[]{:S(2)}) %all-to-all-start.2) | async-done | bytes 2097184 | tf_op jit(solution)/shard_map/all_to_all | solution.py:79
  448.9 1.4 copy.40
  450.2 2.3 dot_general.20
  452.6 10.9 %fusion.46 = (f32[2,256]{1,0:T(2,128)S(1)}, f32[2,256,3072]{2,1,0:T(8,128)S(1)}) fusion(bf16[2,256,2048]{2,1,0:T(8,128)(2,1)} %dot_general.20, bf16[2048,3072]{1,0:T(8,128)(2,1)} %all-gather.2.cloned.1.call-done, f32[2,3072]{1,0:T(2,128)S(1)} %get-tuple-element.189, bf16[1,2,256,3072]{3,2,1,0:T(8,128)(2,1)} %param.20), kind=kOutput, calls=%fused_computation.72 | convolution fusion | flops 6448741888 | bytes 24143872 | tf_op jit(solution)/shard_map/dot_general | solution.py:81
  463.5 0.8 multiply_reduce_fusion
  464.3 1.6 fusion.42
  466.0 1.4 maximum_bitcast_fusion
  467.4 36.1 %pmax.7 = f32[1,2]{1,0:T(1,128)} all-reduce(f32[1,2]{1,0:T(1,128)S(1)} %maximum_bitcast_fusion), channel_id=1, replica_groups=mesh['cfg'=2,'req'=4,'seq'=16] {'seq'}, use_global_device_ids=true, to_apply=%region_16.17 | all-reduce | flops 2 | bytes 16 | tf_op jit(solution)/shard_map/pmax | solution.py:108
  503.4 0.8 multiply_reduce_fusion.1
  504.2 37.3 %psum.7 = f32[2]{0:T(128)S(1)} all-reduce(f32[2]{0:T(128)S(1)} %get-tuple-element.185), channel_id=1, replica_groups=mesh['cfg'=2,'req'=4,'seq'=16] {'seq'}, use_global_device_ids=true, to_apply=%region_13.14 | all-reduce | flops 2 | bytes 16 | tf_op jit(solution)/shard_map/psum | solution.py:107
  (42 shorter events, 3.0 us)
Async XLA Ops:
  7.2 457.1 %copy-start = (bf16[3072,64]{0,1:T(8,128)(2,1)S(1)}, bf16[3072,64]{0,1:T(8,128)(2,1)}, u32[]{:S(2)}) copy-start(bf16[3072,64]{0,1:T(8,128)(2,1)} %param.23) | copy-start | bytes 1179652
  9.4 25.2 %all-to-all-start.1 = ((bf16[2,32,2,16,128]{4,1,2,0,3:T(8,128)(2,1)}), bf16[2,32,2,16,128]{4,1,2,0,3:T(8,128)(2,1)S(1)}, u32[]{:S(2)}, u32[]{:S(2)}) async-start(bf16[2,32,2,16,128]{4,1,2,0,3:T(8,128)(2,1)} %copy.34), calls=%async_computation.1 | async-start | bytes 1048576 | tf_op jit(solution)/shard_map/all_to_all | solution.py:43
  34.6 8.1 %copy-start.6 = (s32[2]{0:T(128)S(1)}, s32[2]{0:T(128)}, u32[]{:S(2)}) copy-start(s32[2]{0:T(128)} %param.16) | copy-start | bytes 28
  34.6 105.1 %all-to-all-start = ((bf16[2,256,3,16,128]{4,1,2,0,3:T(8,128)(2,1)}), bf16[2,256,3,16,128]{4,1,2,0,3:T(8,128)(2,1)}, u32[]{:S(2)}, u32[]{:S(2)}) async-start(bf16[2,256,3,16,128]{4,1,2,0,3:T(8,128)(2,1)} %copy.32), calls=%async_computation | async-start | bytes 12582912 | tf_op jit(solution)/shard_map/all_to_all | solution.py:42
  42.0 410.6 %all-gather.2.cloned.1.call-start = ((), (), s32[]{:S(2)}) async-start(), calls=%async_computation.3 | async-start | bytes 12681216 | tf_op jit(solution)/shard_map/all_gather | solution.py:83
  147.0 122.4 %copy-start.2 = (bf16[512,1,128]{2,0,1:T(8,128)(2,1)S(1)}, bf16[512,1,128]{2,0,1:T(8,128)(2,1)}, u32[]{:S(2)}) copy-start(bf16[512,1,128]{2,0,1:T(8,128)(2,1)} %get-tuple-element.182) | copy-start | bytes 393220
  147.0 122.4 %copy-start.3 = (bf16[512,1,128]{2,0,1:T(8,128)(2,1)S(1)}, bf16[512,1,128]{2,0,1:T(8,128)(2,1)}, u32[]{:S(2)}) copy-start(bf16[512,1,128]{2,0,1:T(8,128)(2,1)} %get-tuple-element.183) | copy-start | bytes 393220
  147.0 125.3 %copy-start.1 = (pred[4608]{0:T(1024)(128)(4,1)S(1)}, pred[4608]{0:T(1024)(128)(4,1)}, u32[]{:S(2)}) copy-start(pred[4608]{0:T(1024)(128)(4,1)} %concatenate.21) | copy-start | bytes 13828
  269.4 2.9 copy-start.9
  394.8 25.2 %copy-start.8 = (s32[2]{0:T(128)S(1)}, s32[2]{0:T(128)}, u32[]{:S(2)}) copy-start(s32[2]{0:T(128)} %param.17) | copy-start | bytes 28
  394.8 25.2 %copy-start.4 = (f32[1,2,3,3072]{3,1,2,0:T(2,128)S(1)}, f32[1,2,3,3072]{3,1,2,0:T(2,128)}, u32[]{:S(2)}) copy-start(f32[1,2,3,3072]{3,1,2,0:T(2,128)} %param.19) | copy-start | bytes 221188
  394.8 25.2 %copy-start.10 = (f32[4]{0:T(128)S(1)}, f32[4]{0:T(128)}, u32[]{:S(2)}) copy-start(f32[4]{0:T(128)} %copy-done.9) | copy-start | bytes 52
  414.6 34.0 %all-to-all-start.2 = ((bf16[2,4096,1,128]{3,0,2,1:T(2,128)(2,1)}), bf16[2,4096,1,128]{3,0,2,1:T(2,128)(2,1)S(1)}, u32[]{:S(2)}, u32[]{:S(2)}) async-start(bf16[2,4096,1,128]{3,0,2,1:T(2,128)(2,1)} %copy.38), calls=%async_computation.2 | async-start | bytes 4194304 | tf_op jit(solution)/shard_map/all_to_all | solution.py:79
  464.3 39.2 %copy-start.5 = (f32[2,256,32]{1,2,0:T(8,128)S(1)}, f32[2,256,32]{1,2,0:T(8,128)}, u32[]{:S(2)}) copy-start(f32[2,256,32]{1,2,0:T(8,128)} %param.21) | copy-start | bytes 196612
  464.3 39.2 %copy-start.7 = (f32[2]{0:T(128)S(1)}, f32[2]{0:T(128)}, u32[]{:S(2)}) copy-start(f32[2]{0:T(128)} %param.18) | copy-start | bytes 28
  465.9 37.5 %collective-permute-start = (f32[2,256,32]{1,2,0:T(8,128)S(1)}, f32[2,256,32]{1,2,0:T(8,128)S(1)}, u32[]{:S(2)}, u32[]{:S(2)}) collective-permute-start(f32[2,256,32]{1,2,0:T(8,128)S(1)} %constant_dynamic-slice_fusion), channel_id=1, source_target_pairs={{0,64},{64,0},{1,65},{65,1},{2,66},{66,2},{3,67},{67,3},{4,68},{68... | collective-permute-start | bytes 196616 | tf_op jit(solution)/shard_map/ppermute | solution.py:15
Sparse Core Ops, SparseCore 0:
  45.9 123.1 all-gather.1
where the time goes:
time: 550 us; the launch traced here: 549 us
  matrix products  154 us (28%)
  waiting for transfers between devices  122 us (22%)
  other arithmetic  109 us (20%)
  blocking collectives  73.4 us (13%)
  local copies, waits for them, and re-layouts  56.1 us (10%)
  starting transfers between devices  20.7 us (4%)
  between operations  14.3 us (3%)
    reduce_max x8, other arithmetic, one_block(): return (mixed_rows, jnp.max(row_max))  97.1 us
    all_to_all x1, waiting for transfers between devices, shards(): lax.all_to_all(joined, 'seq', split_axis=3, concat_axis=1, tiled=True)  93.6 us
    dot_general x8, matrix products, one_block(): jnp.einsum('hqk,khd->qhd', weights, value_rows, preferred_element_type=jn...  74.3 us
    dot_general x8, matrix products, one_block(): jnp.einsum('qhd,khd->hqk', query_rows, key_rows, preferred_element_type=j...  67.2 us
    psum x1, blocking collectives, shards(): total_sq = lax.psum(square_sum, 'seq')  37.3 us
    pmax x1, blocking collectives, shards(): global_max = lax.pmax(local_max, 'seq')  36.1 us
    all_to_all x1, waiting for transfers between devices, shards(): lax.all_to_all(head_rows, 'seq', split_axis=1, concat_axis=2, tiled=True)  27.4 us
    another operation x1, local copies, waits for them, and re-layouts, shards(): head_rows = jnp.stack(mixed_list)  18.4 us
  transfers between devices with their start and end apart: 5, of which 2 were waited for; matrix products, arithmetic and copies ran while one was open for 55% of the time, Pallas kernels for 0%

commit v1 on v0

--- a/solution.py
+++ b/solution.py
@@ -104,7 +104,9 @@
     uncond_vel = jnp.where(is_cond, partner, own_part)
     guided = uncond_vel + guidance[:, None, None] * (cond_vel - uncond_vel)
     square_sum = jnp.sum(guided * guided, axis=(1, 2))
-    total_sq = lax.psum(square_sum, "seq")
+    total_sq = square_sum
+    for hop in (1, 2, 4, 8):
+        total_sq = total_sq + lax.ppermute(total_sq, "seq", [(dev, dev ^ hop) for dev in range(16)])
     global_max = lax.pmax(local_max, "seq")
     vel_norm = jnp.sqrt(total_sq / (img_len * half_chan) + norm_eps)
     euler_step = sigma_of(t_index + 1) - sigma_of(t_index)

time: 550 us -> 531 us (0.965)
  blocking collectives: 73.4 us -> 36.1 us
  waiting for transfers between devices: 122 us -> 137 us
    psum x1 -> x0, blocking collectives: 37.3 us -> none  [shards(): total_sq = lax.psum(square_sum, 'seq')]
    ppermute x0 -> x4, waiting for transfers between devices: none -> 15.4 us  [shards(): lax.ppermute(total_sq, 'seq', [(dev, dev ^ hop) for dev in range(16)])]
  transfers between devices with their start and end apart: 5 -> 9, of which waited for: 2 -> 6; matrix products, arithmetic and copies ran while one was open for 55% -> 57% of each run, Pallas kernels for 0% -> 0%
where the time goes in v1:
time: 531 us; the launch traced here: 529 us
  matrix products  154 us (29%)
  waiting for transfers between devices  137 us (26%)
  other arithmetic  108 us (20%)
  local copies, waits for them, and re-layouts  56 us (11%)
  blocking collectives  36.1 us (7%)
  starting transfers between devices  22.6 us (4%)
  between operations  14.3 us (3%)
    reduce_max x8, other arithmetic, one_block(): return (mixed_rows, jnp.max(row_max))  97.1 us
    all_to_all x1, waiting for transfers between devices, shards(): lax.all_to_all(joined, 'seq', split_axis=3, concat_axis=1, tiled=True)  93.7 us
    dot_general x8, matrix products, one_block(): jnp.einsum('hqk,khd->qhd', weights, value_rows, preferred_element_type=jn...  74.3 us
    dot_general x8, matrix products, one_block(): jnp.einsum('qhd,khd->hqk', query_rows, key_rows, preferred_element_type=j...  67.5 us
    pmax x1, blocking collectives, shards(): global_max = lax.pmax(local_max, 'seq')  36.1 us
    all_to_all x1, waiting for transfers between devices, shards(): lax.all_to_all(head_rows, 'seq', split_axis=1, concat_axis=2, tiled=True)  27.2 us
    another operation x1, local copies, waits for them, and re-layouts, shards(): head_rows = jnp.stack(mixed_list)  18.3 us
    ppermute x4, waiting for transfers between devices, shards(): lax.ppermute(total_sq, 'seq', [(dev, dev ^ hop) for dev in range(16)])  15.4 us
  transfers between devices with their start and end apart: 9, of which 6 were waited for; matrix products, arithmetic and copies ran while one was open for 57% of the time, Pallas kernels for 0%

profile of v1, /device:TPU:24, one launch (start us, length us, event | category | flops | bytes accessed | tf_op | source)
XLA Modules:
  0.0 529.0 jit_solution(12513004892595249120)
XLA Ops:
  7.2 1.2 copy.41
  8.4 1.0 copy.34
  9.4 7.9 %all-to-all-start.1 = ((bf16[2,32,2,16,128]{4,1,2,0,3:T(8,128)(2,1)}), bf16[2,32,2,16,128]{4,1,2,0,3:T(8,128)(2,1)S(1)}, u32[]{:S(2)}, u32[]{:S(2)}) async-start(bf16[2,32,2,16,128]{4,1,2,0,3:T(8,128)(2,1)} %copy.34), calls=%async_computation.1 | async-start | bytes 1048576 | tf_op jit(solution)/shard_map/all_to_all | solution.py:43
  17.3 8.6 %copy.31 = bf16[1,2,256,6144]{2,3,1,0:T(8,128)(2,1)} copy(bf16[1,2,256,6144]{3,2,1,0:T(8,128)(2,1)} %param.14) | data formatting | bytes 12582912 | tf_op args[0]
  25.9 8.6 %copy.32 = bf16[2,256,3,16,128]{4,1,2,0,3:T(8,128)(2,1)} copy(bf16[2,256,3,16,128]{1,4,3,2,0:T(8,128)(2,1)} %bitcast.151) | data formatting | bytes 12582912 | tf_op jit(solution)/shard_map/reshape;squeeze | solution.py:39
  34.6 7.4 %all-to-all-start = ((bf16[2,256,3,16,128]{4,1,2,0,3:T(8,128)(2,1)}), bf16[2,256,3,16,128]{4,1,2,0,3:T(8,128)(2,1)}, u32[]{:S(2)}, u32[]{:S(2)}) async-start(bf16[2,256,3,16,128]{4,1,2,0,3:T(8,128)(2,1)} %copy.32), calls=%async_computation | async-start | bytes 12582912 | tf_op jit(solution)/shard_map/all_to_all | solution.py:42
  45.3 0.7 slice_bitcast_fusion.6
  46.0 93.7 %all-to-all-done = bf16[2,256,3,16,128]{4,1,2,0,3:T(8,128)(2,1)} async-done(((bf16[2,256,3,16,128]{4,1,2,0,3:T(8,128)(2,1)}), bf16[2,256,3,16,128]{4,1,2,0,3:T(8,128)(2,1)}, u32[]{:S(2)}, u32[]{:S(2)}) %all-to-all-start) | async-done | bytes 6291488 | tf_op jit(solution)/shard_map/all_to_all | solution.py:42
  139.7 3.2 copy.33
  142.9 1.7 slice_bitcast_fusion.2
  144.6 1.2 pad_maximum_fusion.1
  145.7 1.1 broadcast.86.clone.1
  146.9 122.6 %while.24 = (s32[]{:T(128)}, bf16[4,1024,1,128]{3,1,2,0:T(8,128)(2,1)}, f32[4]{0:T(128)S(1)}, pred[4608]{0:T(1024)(128)(4,1)S(1)}, bf16[4,1024,1,128]{3,1,2,0:T(...) while((s32[]{:T(128)}, ...), condition=%wide.region_4.5_spmd, body=%wide.region_0.4_spmd.sunk | while | flops 2477389824 | bytes 59542120 | solution.py:71
  146.9 8.2 %fusion.57 = (f32[1024]{0:T(1024)S(1)}, f32[1024,4608]{1,0:T(8,128)}) fusion(pred[4608]{0:T(1024)(128)(4,1)S(1)} %get-tuple-element.343, bf16[4608,1,128]{2,0,1:T(8,128)(2,1)S(1)} %get-tuple-element.345, bf16[4,1024,1,128]{3,1,2,0:T(8,128)(2,1)S(1)} %get-tuple-element.344, s32[]{:T(128)} %get-tuple-element.332), kind=kOutput, calls=%fused_computation.5.clone.1 | convolution fusion | flops 1222114304 | bytes 20325380 | tf_op jit(solution)/shard_map/while/body/eval_jaxpr/qhd,khd->hqk/dot_general | solution.py:59
  155.1 13.3 %fusion.58 = (f32[]{:T(128)}, f32[1024]{0:T(1024)S(1)}) fusion(f32[1024,4608]{1,0:T(8,128)} %get-tuple-element.285, pred[4608]{0:T(1024)(128)(4,1)S(1)} %get-tuple-element.343, f32[1024]{0:T(1024)S(1)} %get-tuple-element.286), kind=kLoop, calls=%fused_computation.4.clone.1 | loop fusion | flops 23591936 | bytes 18887172 | tf_op jit(solution)/shard_map/while/body/eval_jaxpr/reduce_max | solution.py:69
  168.4 9.6 %fusion.59 = bf16[4,1024,1,128]{3,1,2,0:T(8,128)(2,1)} fusion(bf16[4,1024,1,128]{3,1,2,0:T(8,128)(2,1)} %get-tuple-element.333, s32[]{:T(128)} %get-tuple-element.332, bf16[4608,1,128]{2,0,1:T(8,128)(2,1)} %get-tuple-element.346, f32[1024,4608]{1,0:T(8,128)} %get-tuple-element.285, f32[1024]{0:T(1024)S(1)} %get-tuple-element.287, ...), kind=kOutput, calls=%fused_computation.12.clone.1 | convolution fusion | flops 1231683584 | bytes 20329472 | tf_op jit(solution)/shard_map/while/body/eval_jaxpr/hqk,khd->qhd/dot_general | solution.py:66
  178.0 0.8 dynamic_update_slice.21
  178.7 7.9 %fusion.57 = (f32[1024]{0:T(1024)S(1)}, f32[1024,4608]{1,0:T(8,128)}) fusion(pred[4608]{0:T(1024)(128)(4,1)S(1)} %get-tuple-element.343, bf16[4608,1,128]{2,0,1:T(8,128)(2,1)S(1)} %get-tuple-element.345, bf16[4,1024,1,128]{3,1,2,0:T(8,128)(2,1)S(1)} %get-tuple-element.344, s32[]{:T(128)} %get-tuple-element.332), kind=kOutput, calls=%fused_computation.5.clone.1 | convolution fusion | flops 1222114304 | bytes 20325380 | tf_op jit(solution)/shard_map/while/body/eval_jaxpr/qhd,khd->hqk/dot_general | solution.py:59
  186.7 12.0 %fusion.58 = (f32[]{:T(128)}, f32[1024]{0:T(1024)S(1)}) fusion(f32[1024,4608]{1,0:T(8,128)} %get-tuple-element.285, pred[4608]{0:T(1024)(128)(4,1)S(1)} %get-tuple-element.343, f32[1024]{0:T(1024)S(1)} %get-tuple-element.286), kind=kLoop, calls=%fused_computation.4.clone.1 | loop fusion | flops 23591936 | bytes 18887172 | tf_op jit(solution)/shard_map/while/body/eval_jaxpr/reduce_max | solution.py:69
  198.7 9.6 %fusion.59 = bf16[4,1024,1,128]{3,1,2,0:T(8,128)(2,1)} fusion(bf16[4,1024,1,128]{3,1,2,0:T(8,128)(2,1)} %get-tuple-element.333, s32[]{:T(128)} %get-tuple-element.332, bf16[4608,1,128]{2,0,1:T(8,128)(2,1)} %get-tuple-element.346, f32[1024,4608]{1,0:T(8,128)} %get-tuple-element.285, f32[1024]{0:T(1024)S(1)} %get-tuple-element.287, ...), kind=kOutput, calls=%fused_computation.12.clone.1 | convolution fusion | flops 1231683584 | bytes 20329472 | tf_op jit(solution)/shard_map/while/body/eval_jaxpr/hqk,khd->qhd/dot_general | solution.py:66
  208.2 0.8 dynamic_update_slice.21
  209.0 7.9 %fusion.57 = (f32[1024]{0:T(1024)S(1)}, f32[1024,4608]{1,0:T(8,128)}) fusion(pred[4608]{0:T(1024)(128)(4,1)S(1)} %get-tuple-element.343, bf16[4608,1,128]{2,0,1:T(8,128)(2,1)S(1)} %get-tuple-element.345, bf16[4,1024,1,128]{3,1,2,0:T(8,128)(2,1)S(1)} %get-tuple-element.344, s32[]{:T(128)} %get-tuple-element.332), kind=kOutput, calls=%fused_computation.5.clone.1 | convolution fusion | flops 1222114304 | bytes 20325380 | tf_op jit(solution)/shard_map/while/body/eval_jaxpr/qhd,khd->hqk/dot_general | solution.py:59
  216.9 12.0 %fusion.58 = (f32[]{:T(128)}, f32[1024]{0:T(1024)S(1)}) fusion(f32[1024,4608]{1,0:T(8,128)} %get-tuple-element.285, pred[4608]{0:T(1024)(128)(4,1)S(1)} %get-tuple-element.343, f32[1024]{0:T(1024)S(1)} %get-tuple-element.286), kind=kLoop, calls=%fused_computation.4.clone.1 | loop fusion | flops 23591936 | bytes 18887172 | tf_op jit(solution)/shard_map/while/body/eval_jaxpr/reduce_max | solution.py:69
  228.9 9.6 %fusion.59 = bf16[4,1024,1,128]{3,1,2,0:T(8,128)(2,1)} fusion(bf16[4,1024,1,128]{3,1,2,0:T(8,128)(2,1)} %get-tuple-element.333, s32[]{:T(128)} %get-tuple-element.332, bf16[4608,1,128]{2,0,1:T(8,128)(2,1)} %get-tuple-element.346, f32[1024,4608]{1,0:T(8,128)} %get-tuple-element.285, f32[1024]{0:T(1024)S(1)} %get-tuple-element.287, ...), kind=kOutput, calls=%fused_computation.12.clone.1 | convolution fusion | flops 1231683584 | bytes 20329472 | tf_op jit(solution)/shard_map/while/body/eval_jaxpr/hqk,khd->qhd/dot_general | solution.py:66
  238.5 0.8 dynamic_update_slice.21
  239.2 7.9 %fusion.57 = (f32[1024]{0:T(1024)S(1)}, f32[1024,4608]{1,0:T(8,128)}) fusion(pred[4608]{0:T(1024)(128)(4,1)S(1)} %get-tuple-element.343, bf16[4608,1,128]{2,0,1:T(8,128)(2,1)S(1)} %get-tuple-element.345, bf16[4,1024,1,128]{3,1,2,0:T(8,128)(2,1)S(1)} %get-tuple-element.344, s32[]{:T(128)} %get-tuple-element.332), kind=kOutput, calls=%fused_computation.5.clone.1 | convolution fusion | flops 1222114304 | bytes 20325380 | tf_op jit(solution)/shard_map/while/body/eval_jaxpr/qhd,khd->hqk/dot_general | solution.py:59
  247.2 12.0 %fusion.58 = (f32[]{:T(128)}, f32[1024]{0:T(1024)S(1)}) fusion(f32[1024,4608]{1,0:T(8,128)} %get-tuple-element.285, pred[4608]{0:T(1024)(128)(4,1)S(1)} %get-tuple-element.343, f32[1024]{0:T(1024)S(1)} %get-tuple-element.286), kind=kLoop, calls=%fused_computation.4.clone.1 | loop fusion | flops 23591936 | bytes 18887172 | tf_op jit(solution)/shard_map/while/body/eval_jaxpr/reduce_max | solution.py:69
  259.1 9.6 %fusion.59 = bf16[4,1024,1,128]{3,1,2,0:T(8,128)(2,1)} fusion(bf16[4,1024,1,128]{3,1,2,0:T(8,128)(2,1)} %get-tuple-element.333, s32[]{:T(128)} %get-tuple-element.332, bf16[4608,1,128]{2,0,1:T(8,128)(2,1)} %get-tuple-element.346, f32[1024,4608]{1,0:T(8,128)} %get-tuple-element.285, f32[1024]{0:T(1024)S(1)} %get-tuple-element.287, ...), kind=kOutput, calls=%fused_computation.12.clone.1 | convolution fusion | flops 1231683584 | bytes 20329472 | tf_op jit(solution)/shard_map/while/body/eval_jaxpr/hqk,khd->qhd/dot_general | solution.py:66
  268.7 0.8 dynamic_update_slice.21
  269.5 2.7 pad_maximum_fusion.3
  272.4 122.6 %while.25 = (s32[]{:T(128)}, bf16[4,1024,1,128]{3,1,2,0:T(8,128)(2,1)S(1)}, f32[4]{0:T(128)S(1)}, pred[4608]{0:T(1024)(128)(4,1)S(1)}, bf16[4,1024,1,128]{3,1,2,...) while((s32[]{:T(128)}, ...), condition=%wide.region_9.10_spmd, body=%wide.region_5.9_spmd.sunk | while | flops 2477389824 | bytes 59542120 | solution.py:71
  272.6 8.9 %fusion.61 = (f32[1024]{0:T(1024)S(1)}, f32[1024,4608]{1,0:T(8,128)}) fusion(pred[4608]{0:T(1024)(128)(4,1)S(1)} %get-tuple-element.319, bf16[4608,1,128]{2,0,1:T(8,128)(2,1)S(1)} %get-tuple-element.321, bf16[4,1024,1,128]{3,1,2,0:T(8,128)(2,1)} %get-tuple-element.320, s32[]{:T(128)} %get-tuple-element.308), kind=kOutput, calls=%fused_computation.23.clone.1 | convolution fusion | flops 1222114304 | bytes 20325376 | tf_op jit(solution)/shard_map/while/body/eval_jaxpr/qhd,khd->hqk/dot_general | solution.py:59
  281.5 12.0 %fusion.62 = (f32[]{:T(128)}, f32[1024]{0:T(1024)S(1)}) fusion(f32[1024,4608]{1,0:T(8,128)} %get-tuple-element.296, pred[4608]{0:T(1024)(128)(4,1)S(1)} %get-tuple-element.319, f32[1024]{0:T(1024)S(1)} %get-tuple-element.297), kind=kLoop, calls=%fused_computation.22.clone.1 | loop fusion | flops 23591936 | bytes 18887172 | tf_op jit(solution)/shard_map/while/body/eval_jaxpr/reduce_max | solution.py:69
  293.4 9.0 %fusion.63 = bf16[4,1024,1,128]{3,1,2,0:T(8,128)(2,1)S(1)} fusion(bf16[4,1024,1,128]{3,1,2,0:T(8,128)(2,1)S(1)} %get-tuple-element.309, s32[]{:T(128)} %get-tuple-element.308, bf16[4608,1,128]{2,0,1:T(8,128)(2,1)} %get-tuple-element.322, f32[1024,4608]{1,0:T(8,128)} %get-tuple-element.296, f32[1024]{0:T(1024)S(1)} %get-tuple-element.298, ...), kind=kOutput, calls=%fused_computation.30.clone.1 | convolution fusion | flops 1231683584 | bytes 20329476 | tf_op jit(solution)/shard_map/while/body/eval_jaxpr/hqk,khd->qhd/dot_general | solution.py:66
  302.4 0.8 dynamic_update_slice.23
  303.2 8.9 %fusion.61 = (f32[1024]{0:T(1024)S(1)}, f32[1024,4608]{1,0:T(8,128)}) fusion(pred[4608]{0:T(1024)(128)(4,1)S(1)} %get-tuple-element.319, bf16[4608,1,128]{2,0,1:T(8,128)(2,1)S(1)} %get-tuple-element.321, bf16[4,1024,1,128]{3,1,2,0:T(8,128)(2,1)} %get-tuple-element.320, s32[]{:T(128)} %get-tuple-element.308), kind=kOutput, calls=%fused_computation.23.clone.1 | convolution fusion | flops 1222114304 | bytes 20325376 | tf_op jit(solution)/shard_map/while/body/eval_jaxpr/qhd,khd->hqk/dot_general | solution.py:59
  312.1 12.0 %fusion.62 = (f32[]{:T(128)}, f32[1024]{0:T(1024)S(1)}) fusion(f32[1024,4608]{1,0:T(8,128)} %get-tuple-element.296, pred[4608]{0:T(1024)(128)(4,1)S(1)} %get-tuple-element.319, f32[1024]{0:T(1024)S(1)} %get-tuple-element.297), kind=kLoop, calls=%fused_computation.22.clone.1 | loop fusion | flops 23591936 | bytes 18887172 | tf_op jit(solution)/shard_map/while/body/eval_jaxpr/reduce_max | solution.py:69
  324.1 9.0 %fusion.63 = bf16[4,1024,1,128]{3,1,2,0:T(8,128)(2,1)S(1)} fusion(bf16[4,1024,1,128]{3,1,2,0:T(8,128)(2,1)S(1)} %get-tuple-element.309, s32[]{:T(128)} %get-tuple-element.308, bf16[4608,1,128]{2,0,1:T(8,128)(2,1)} %get-tuple-element.322, f32[1024,4608]{1,0:T(8,128)} %get-tuple-element.296, f32[1024]{0:T(1024)S(1)} %get-tuple-element.298, ...), kind=kOutput, calls=%fused_computation.30.clone.1 | convolution fusion | flops 1231683584 | bytes 20329476 | tf_op jit(solution)/shard_map/while/body/eval_jaxpr/hqk,khd->qhd/dot_general | solution.py:66
  333.0 0.8 dynamic_update_slice.23
  333.8 8.9 %fusion.61 = (f32[1024]{0:T(1024)S(1)}, f32[1024,4608]{1,0:T(8,128)}) fusion(pred[4608]{0:T(1024)(128)(4,1)S(1)} %get-tuple-element.319, bf16[4608,1,128]{2,0,1:T(8,128)(2,1)S(1)} %get-tuple-element.321, bf16[4,1024,1,128]{3,1,2,0:T(8,128)(2,1)} %get-tuple-element.320, s32[]{:T(128)} %get-tuple-element.308), kind=kOutput, calls=%fused_computation.23.clone.1 | convolution fusion | flops 1222114304 | bytes 20325376 | tf_op jit(solution)/shard_map/while/body/eval_jaxpr/qhd,khd->hqk/dot_general | solution.py:59
  342.7 12.0 %fusion.62 = (f32[]{:T(128)}, f32[1024]{0:T(1024)S(1)}) fusion(f32[1024,4608]{1,0:T(8,128)} %get-tuple-element.296, pred[4608]{0:T(1024)(128)(4,1)S(1)} %get-tuple-element.319, f32[1024]{0:T(1024)S(1)} %get-tuple-element.297), kind=kLoop, calls=%fused_computation.22.clone.1 | loop fusion | flops 23591936 | bytes 18887172 | tf_op jit(solution)/shard_map/while/body/eval_jaxpr/reduce_max | solution.py:69
  354.7 9.0 %fusion.63 = bf16[4,1024,1,128]{3,1,2,0:T(8,128)(2,1)S(1)} fusion(bf16[4,1024,1,128]{3,1,2,0:T(8,128)(2,1)S(1)} %get-tuple-element.309, s32[]{:T(128)} %get-tuple-element.308, bf16[4608,1,128]{2,0,1:T(8,128)(2,1)} %get-tuple-element.322, f32[1024,4608]{1,0:T(8,128)} %get-tuple-element.296, f32[1024]{0:T(1024)S(1)} %get-tuple-element.298, ...), kind=kOutput, calls=%fused_computation.30.clone.1 | convolution fusion | flops 1231683584 | bytes 20329476 | tf_op jit(solution)/shard_map/while/body/eval_jaxpr/hqk,khd->qhd/dot_general | solution.py:66
  363.7 0.8 dynamic_update_slice.23
  364.4 8.9 %fusion.61 = (f32[1024]{0:T(1024)S(1)}, f32[1024,4608]{1,0:T(8,128)}) fusion(pred[4608]{0:T(1024)(128)(4,1)S(1)} %get-tuple-element.319, bf16[4608,1,128]{2,0,1:T(8,128)(2,1)S(1)} %get-tuple-element.321, bf16[4,1024,1,128]{3,1,2,0:T(8,128)(2,1)} %get-tuple-element.320, s32[]{:T(128)} %get-tuple-element.308), kind=kOutput, calls=%fused_computation.23.clone.1 | convolution fusion | flops 1222114304 | bytes 20325376 | tf_op jit(solution)/shard_map/while/body/eval_jaxpr/qhd,khd->hqk/dot_general | solution.py:59
  373.3 12.0 %fusion.62 = (f32[]{:T(128)}, f32[1024]{0:T(1024)S(1)}) fusion(f32[1024,4608]{1,0:T(8,128)} %get-tuple-element.296, pred[4608]{0:T(1024)(128)(4,1)S(1)} %get-tuple-element.319, f32[1024]{0:T(1024)S(1)} %get-tuple-element.297), kind=kLoop, calls=%fused_computation.22.clone.1 | loop fusion | flops 23591936 | bytes 18887172 | tf_op jit(solution)/shard_map/while/body/eval_jaxpr/reduce_max | solution.py:69
  385.3 9.0 %fusion.63 = bf16[4,1024,1,128]{3,1,2,0:T(8,128)(2,1)S(1)} fusion(bf16[4,1024,1,128]{3,1,2,0:T(8,128)(2,1)S(1)} %get-tuple-element.309, s32[]{:T(128)} %get-tuple-element.308, bf16[4608,1,128]{2,0,1:T(8,128)(2,1)} %get-tuple-element.322, f32[1024,4608]{1,0:T(8,128)} %get-tuple-element.296, f32[1024]{0:T(1024)S(1)} %get-tuple-element.298, ...), kind=kOutput, calls=%fused_computation.30.clone.1 | convolution fusion | flops 1231683584 | bytes 20329476 | tf_op jit(solution)/shard_map/while/body/eval_jaxpr/hqk,khd->qhd/dot_general | solution.py:66
  394.3 0.8 dynamic_update_slice.23
  395.0 1.5 pad_maximum_fusion
  396.5 18.3 %copy.38 = bf16[2,4096,1,128]{3,0,2,1:T(2,128)(2,1)} copy(bf16[2,4096,1,128]{3,1,2,0:T(8,128)(2,1)S(1)} %pad_maximum_fusion) | data formatting | bytes 4194304 | tf_op jit(solution)/shard_map/stack | solution.py:78
  414.8 5.4 %all-to-all-start.2 = ((bf16[2,4096,1,128]{3,0,2,1:T(2,128)(2,1)}), bf16[2,4096,1,128]{3,0,2,1:T(2,128)(2,1)S(1)}, u32[]{:S(2)}, u32[]{:S(2)}) async-start(bf16[2,4096,1,128]{3,0,2,1:T(2,128)(2,1)} %copy.38), calls=%async_computation.2 | async-start | bytes 4194304 | tf_op jit(solution)/shard_map/all_to_all | solution.py:79
  421.5 27.2 %all-to-all-done.2 = bf16[2,4096,1,128]{3,0,2,1:T(2,128)(2,1)S(1)} async-done(((bf16[2,4096,1,128]{3,0,2,1:T(2,128)(2,1)}), bf16[2,4096,1,128]{3,0,2,1:T(2,128)(2,1)S(1)}, u32[]{:S(2)}, u32[]{:S(2)}) %all-to-all-start.2) | async-done | bytes 2097184 | tf_op jit(solution)/shard_map/all_to_all | solution.py:79
  449.0 1.4 copy.40
  450.4 2.3 dot_general.20
  452.6 10.9 %fusion.46 = (f32[2,256]{1,0:T(2,128)S(1)}, f32[2,256,3072]{2,1,0:T(8,128)S(1)}) fusion(bf16[2,256,2048]{2,1,0:T(8,128)(2,1)} %dot_general.20, bf16[2048,3072]{1,0:T(8,128)(2,1)} %all-gather.2.cloned.1.call-done, f32[2,3072]{1,0:T(2,128)S(1)} %get-tuple-element.189, bf16[1,2,256,3072]{3,2,1,0:T(8,128)(2,1)} %param.20), kind=kOutput, calls=%fused_computation.72 | convolution fusion | flops 6448741888 | bytes 24143872 | tf_op jit(solution)/shard_map/dot_general | solution.py:81
  463.6 0.8 multiply_reduce_fusion
  464.4 1.6 fusion.42
  466.1 1.4 maximum_bitcast_fusion
  467.4 36.1 %pmax.7 = f32[1,2]{1,0:T(1,128)} all-reduce(f32[1,2]{1,0:T(1,128)S(1)} %maximum_bitcast_fusion), channel_id=1, replica_groups=mesh['cfg'=2,'req'=4,'seq'=16] {'seq'}, use_global_device_ids=true, to_apply=%region_15.16 | all-reduce | flops 2 | bytes 16 | tf_op jit(solution)/shard_map/pmax | solution.py:110
  503.5 0.8 multiply_reduce_fusion.1
  504.3 1.9 collective-permute-start.1
  506.2 1.7 collective-permute-done.1
  507.9 5.1 collective-permute-done.2
  513.0 3.6 collective-permute-done.3
  516.6 5.1 collective-permute-done.4
  (52 shorter events, 5.6 us)
Async XLA Ops:
  7.2 457.2 %copy-start = (bf16[3072,64]{0,1:T(8,128)(2,1)S(1)}, bf16[3072,64]{0,1:T(8,128)(2,1)}, u32[]{:S(2)}) copy-start(bf16[3072,64]{0,1:T(8,128)(2,1)} %param.23) | copy-start | bytes 1179652
  9.4 25.2 %all-to-all-start.1 = ((bf16[2,32,2,16,128]{4,1,2,0,3:T(8,128)(2,1)}), bf16[2,32,2,16,128]{4,1,2,0,3:T(8,128)(2,1)S(1)}, u32[]{:S(2)}, u32[]{:S(2)}) async-start(bf16[2,32,2,16,128]{4,1,2,0,3:T(8,128)(2,1)} %copy.34), calls=%async_computation.1 | async-start | bytes 1048576 | tf_op jit(solution)/shard_map/all_to_all | solution.py:43
  34.5 8.1 %copy-start.6 = (s32[2]{0:T(128)S(1)}, s32[2]{0:T(128)}, u32[]{:S(2)}) copy-start(s32[2]{0:T(128)} %param.16) | copy-start | bytes 28
  34.6 105.1 %all-to-all-start = ((bf16[2,256,3,16,128]{4,1,2,0,3:T(8,128)(2,1)}), bf16[2,256,3,16,128]{4,1,2,0,3:T(8,128)(2,1)}, u32[]{:S(2)}, u32[]{:S(2)}) async-start(bf16[2,256,3,16,128]{4,1,2,0,3:T(8,128)(2,1)} %copy.32), calls=%async_computation | async-start | bytes 12582912 | tf_op jit(solution)/shard_map/all_to_all | solution.py:42
  42.0 410.7 %all-gather.2.cloned.1.call-start = ((), (), s32[]{:S(2)}) async-start(), calls=%async_computation.3 | async-start | bytes 12681216 | tf_op jit(solution)/shard_map/all_gather | solution.py:83
  146.9 122.6 %copy-start.2 = (bf16[512,1,128]{2,0,1:T(8,128)(2,1)S(1)}, bf16[512,1,128]{2,0,1:T(8,128)(2,1)}, u32[]{:S(2)}) copy-start(bf16[512,1,128]{2,0,1:T(8,128)(2,1)} %get-tuple-element.182) | copy-start | bytes 393220
  146.9 122.6 %copy-start.3 = (bf16[512,1,128]{2,0,1:T(8,128)(2,1)S(1)}, bf16[512,1,128]{2,0,1:T(8,128)(2,1)}, u32[]{:S(2)}) copy-start(bf16[512,1,128]{2,0,1:T(8,128)(2,1)} %get-tuple-element.183) | copy-start | bytes 393220
  146.9 125.5 %copy-start.1 = (pred[4608]{0:T(1024)(128)(4,1)S(1)}, pred[4608]{0:T(1024)(128)(4,1)}, u32[]{:S(2)}) copy-start(pred[4608]{0:T(1024)(128)(4,1)} %concatenate.21) | copy-start | bytes 13828
  269.5 2.9 copy-start.9
  395.0 25.2 %copy-start.8 = (s32[2]{0:T(128)S(1)}, s32[2]{0:T(128)}, u32[]{:S(2)}) copy-start(s32[2]{0:T(128)} %param.17) | copy-start | bytes 28
  395.0 25.2 %copy-start.4 = (f32[1,2,3,3072]{3,1,2,0:T(2,128)S(1)}, f32[1,2,3,3072]{3,1,2,0:T(2,128)}, u32[]{:S(2)}) copy-start(f32[1,2,3,3072]{3,1,2,0:T(2,128)} %param.19) | copy-start | bytes 221188
  395.0 25.2 %copy-start.10 = (f32[4]{0:T(128)S(1)}, f32[4]{0:T(128)}, u32[]{:S(2)}) copy-start(f32[4]{0:T(128)} %copy-done.9) | copy-start | bytes 52
  414.8 33.9 %all-to-all-start.2 = ((bf16[2,4096,1,128]{3,0,2,1:T(2,128)(2,1)}), bf16[2,4096,1,128]{3,0,2,1:T(2,128)(2,1)S(1)}, u32[]{:S(2)}, u32[]{:S(2)}) async-start(bf16[2,4096,1,128]{3,0,2,1:T(2,128)(2,1)} %copy.38), calls=%async_computation.2 | async-start | bytes 4194304 | tf_op jit(solution)/shard_map/all_to_all | solution.py:79
  464.3 39.2 %copy-start.5 = (f32[2,256,32]{1,2,0:T(8,128)S(1)}, f32[2,256,32]{1,2,0:T(8,128)}, u32[]{:S(2)}) copy-start(f32[2,256,32]{1,2,0:T(8,128)} %param.21) | copy-start | bytes 196612
  464.4 39.2 %copy-start.7 = (f32[2]{0:T(128)S(1)}, f32[2]{0:T(128)}, u32[]{:S(2)}) copy-start(f32[2]{0:T(128)} %param.18) | copy-start | bytes 28
  466.0 37.5 %collective-permute-start = (f32[2,256,32]{1,2,0:T(8,128)S(1)}, f32[2,256,32]{1,2,0:T(8,128)S(1)}, u32[]{:S(2)}, u32[]{:S(2)}) collective-permute-start(f32[2,256,32]{1,2,0:T(8,128)S(1)} %constant_dynamic-slice_fusion), channel_id=1, source_target_pairs={{0,64},{64,0},{1,65},{65,1},{2,66},{66,2},{3,67},{67,3},{4,68},{68... | collective-permute-start | bytes 196616 | tf_op jit(solution)/shard_map/ppermute | solution.py:15
  504.3 3.6 collective-permute-start.1
  507.9 5.1 collective-permute-start.2
  513.0 3.6 collective-permute-start.3
  516.6 5.1 collective-permute-start.4
Sparse Core Ops, SparseCore 0:
  45.9 123.1 all-gather.1
